TPU v7x, 512 devices: a whole 4x4x16 slice. The times are simulated.
512 devices in a mesh: seq: 16 (over z), head: 32 (over x, y, core).
Axes of the slice: x: 4, y: 4, z: 16, core: 2. Of those that a mesh axis runs over, the one named last changes fastest.
Arguments:
- queries: bfloat16 [16384, 8192], P('seq', 'head'), may hold values from -6 to 6
- keys: bfloat16 [16384, 8192], P('seq', 'head'), may hold values from -1 to 1
- values: bfloat16 [16384, 8192], P('seq', 'head'), may hold values from -40 to 40
- log_decay: float32 [64, 16384], P('head', 'seq'), may hold values from -1 to 0
- gain: float32 [8192], P('head'), may hold values from 0.25 to 1.75
- out_grad: bfloat16 [16384, 8192], P('seq', 'head'), may hold values from -16 to 16
Outputs:
- output: bfloat16 [16384, 8192], P('seq', 'head')
- query_grad: bfloat16 [16384, 8192], P('seq', 'head')
- key_grad: bfloat16 [16384, 8192], P('seq', 'head')
- value_grad: bfloat16 [16384, 8192], P('seq', 'head')
- gain_grad: float32 [8192], P('head')
All inputs are finite; a program needn't handle non-finite values.
Results may differ from a plain program's by a relative error of at most 0.001.
Values sent between devices are 32-bit elements; how exact they have to be, the bound alone decides.
No kernel may reach another device: no remote copies, remote signals or barrier semaphores. Data moves between devices by JAX's collectives and lax.ppermute only.
A program may use at most 64 MiB of HBM per device.

v0:
```python
import jax
import jax.numpy as jnp
from jax import lax
from jax.sharding import PartitionSpec as P

epsilon = 1e-06
highest = lax.Precision.HIGHEST


def passed_along(value, axis, steps):
    count = lax.axis_size(axis)
    initial, last = (max(0, -steps), min(count, count - steps))
    return lax.ppermute(value, axis, [(source, source + steps) for source in range(initial, last)])


def to_blocks(matrix, heads_local, block_count, block_rows):
    head_width = matrix.shape[1] // heads_local
    return matrix.reshape(block_count, block_rows, heads_local, head_width).transpose(2, 0, 1, 3)


def from_blocks(blocked):
    heads_local, block_count, block_rows, head_width = blocked.shape
    return blocked.transpose(1, 2, 0, 3).reshape(block_count * block_rows, heads_local * head_width)


def carry_forward(device_decay, device_state):

    def relay_step(iteration, prefix):
        outgoing = jnp.exp(device_decay)[:, None, None] * prefix + device_state
        return passed_along(outgoing, "seq", 1)

    return lax.fori_loop(0, lax.axis_size("seq") - 1, relay_step, jnp.zeros_like(device_state))


def carry_backward(device_decay, device_back):

    def relay_step(iteration, suffix):
        outgoing = jnp.exp(device_decay)[:, None, None] * suffix + device_back
        return passed_along(outgoing, "seq", -1)

    return lax.fori_loop(0, lax.axis_size("seq") - 1, relay_step, jnp.zeros_like(device_back))


def local(queries, keys, values, log_decay, gain, out_grad):
    token_rows, channels = queries.shape
    heads_local = log_decay.shape[0]
    block_rows = min(256, token_rows)
    block_count = token_rows // block_rows
    total_channels = channels * lax.axis_size("head")
    query_narrow = to_blocks(queries, heads_local, block_count, block_rows)
    key_narrow = to_blocks(keys, heads_local, block_count, block_rows)
    query_blocks = query_narrow.astype(jnp.float32)
    key_blocks = key_narrow.astype(jnp.float32)
    value_blocks = to_blocks(values, heads_local, block_count, block_rows).astype(jnp.float32)
    decay_sum = jnp.cumsum(log_decay.reshape(heads_local, block_count, block_rows), axis=2)
    block_total = decay_sum[:, :, -1]
    causal = jnp.arange(block_rows)[:, None] >= jnp.arange(block_rows)[None, :]
    mask_decay = jnp.exp(
        jnp.where(causal, decay_sum[..., :, None] - decay_sum[..., None, :], -1e30)
    )
    from_start = jnp.exp(decay_sum)[..., None]
    to_end = jnp.exp(block_total[..., None] - decay_sum)[..., None]
    scores = (
        jnp.einsum("hnid,hnjd->hnij", query_narrow, key_narrow, preferred_element_type=jnp.float32)
        * mask_decay
    )
    inside = jnp.einsum("hnij,hnjd->hnid", scores, value_blocks, precision=highest)
    own_states = jnp.einsum("hnjd,hnje->hnde", key_blocks * to_end, value_blocks, precision=highest)
    device_decay = jnp.sum(block_total, axis=1)
    device_state = jnp.zeros_like(own_states[:, 0])
    for block_index in range(block_count):
        device_state = (
            jnp.exp(block_total[:, block_index])[:, None, None] * device_state
            + own_states[:, block_index]
        )
    incoming = carry_forward(device_decay, device_state)
    entering = []
    running = incoming
    for block_index in range(block_count):
        entering.append(running)
        running = (
            jnp.exp(block_total[:, block_index])[:, None, None] * running
            + own_states[:, block_index]
        )
    entering = jnp.stack(entering, axis=1)
    attended = inside + from_start * jnp.einsum(
        "hnid,hnde->hnie", query_blocks, entering, precision=highest
    )
    flattened = from_blocks(attended)
    grad_wide = out_grad.astype(jnp.float32)
    normed_grad = grad_wide * gain
    squares = lax.psum(jnp.sum(flattened * flattened, axis=1), "head")
    inverse = 1.0 / jnp.sqrt(squares / total_channels + epsilon)
    normed = flattened * inverse[:, None]
    projected = lax.psum(jnp.sum(normed_grad * normed, axis=1), "head")
    output = (normed * gain).astype(jnp.bfloat16)
    gain_part = jnp.sum(grad_wide * normed, axis=0)
    flat_grad = (normed_grad - normed * (projected / total_channels)[:, None]) * inverse[:, None]
    attended_grad = to_blocks(flat_grad, heads_local, block_count, block_rows)
    score_grad = (
        jnp.einsum("hnid,hnjd->hnij", attended_grad, value_blocks, precision=highest) * mask_decay
    )
    query_grad = jnp.einsum("hnij,hnjd->hnid", score_grad, key_blocks, precision=highest)
    query_grad = query_grad + from_start * jnp.einsum(
        "hnie,hnde->hnid", attended_grad, entering, precision=highest
    )
    key_grad = jnp.einsum("hnij,hnid->hnjd", score_grad, query_blocks, precision=highest)
    value_grad = jnp.einsum("hnij,hnid->hnjd", scores, attended_grad, precision=highest)
    own_back = jnp.einsum(
        "hnid,hnie->hnde", query_blocks * from_start, attended_grad, precision=highest
    )
    device_back = jnp.zeros_like(device_state)
    for block_index in reversed(range(block_count)):
        device_back = (
            own_back[:, block_index]
            + jnp.exp(block_total[:, block_index])[:, None, None] * device_back
        )
    later_sum = carry_backward(device_decay, device_back)
    leaving = []
    running = later_sum
    for block_index in reversed(range(block_count)):
        leaving.append(running)
        running = (
            own_back[:, block_index] + jnp.exp(block_total[:, block_index])[:, None, None] * running
        )
    leaving = jnp.stack(leaving[::-1], axis=1)
    key_grad = key_grad + to_end * jnp.einsum(
        "hnje,hnde->hnjd", value_blocks, leaving, precision=highest
    )
    value_grad = value_grad + to_end * jnp.einsum(
        "hnjd,hnde->hnje", key_blocks, leaving, precision=highest
    )
    gain_grad = lax.psum(gain_part, "seq")
    return (
        output,
        from_blocks(query_grad).astype(jnp.bfloat16),
        from_blocks(key_grad).astype(jnp.bfloat16),
        from_blocks(value_grad).astype(jnp.bfloat16),
        gain_grad,
    )


def solution(mesh):
    in_specs = (
        P("seq", "head"),
        P("seq", "head"),
        P("seq", "head"),
        P("head", "seq"),
        P("head"),
        P("seq", "head"),
    )
    out_specs = (P("seq", "head"), P("seq", "head"), P("seq", "head"), P("seq", "head"), P("head"))
    return jax.shard_map(local, mesh=mesh, in_specs=in_specs, out_specs=out_specs, check_vma=False)
```

profile of v0, /device:TPU:96, one launch (start us, length us, event | category | flops | bytes accessed | tf_op | source)
XLA Modules:
  0.0 471.4 jit_solution(15646903390274113141)
XLA Ops:
  9.9 125.4 %while.24 = (s32[]{:T(128)}, f32[2,128,128]{2,1,0:T(8,128)S(1)}, f32[2,1,1]{0,2,1:T(1,128)S(1)}, f32[2,128,128]{2,1,0:T(8,128)S(1)}, s32[]{:T(128)}) while((s32[]{:T(128)}, f32[2,128,128]{2,1,0:T(8,128)S(1)}, f32[2,1,1]{0,2,1:T(1,128)S(1)}, f32[2,128,128]{2,1,0:T(8,128)S(1)}, s32[]{:T(128)}) %tuple.63), condition=%wide.region_4.5_spmd, body=%wide.region_3.4_spmd.sunk | while | flops 65538 | bytes 917613 | solution.py:32
  17.8 5.6 %collective-permute-start = (f32[2,128,128]{2,1,0:T(8,128)S(1)}, f32[2,128,128]{2,1,0:T(8,128)S(1)}, u32[]{:S(2)}, u32[]{:S(2)}) collective-permute-start(f32[2,128,128]{2,1,0:T(8,128)S(1)} %multiply_add_fusion.10), channel_id=1, source_target_pairs={{0,32},{32,64},{64,96},{96,128},{128,160},{160,192},{192,224},{224... | collective-permute-start | bytes 393224 | tf_op jit(solution)/shard_map/while/body/eval_jaxpr/ppermute | solution.py:13
  59.6 5.6 %collective-permute-start = (f32[2,128,128]{2,1,0:T(8,128)S(1)}, f32[2,128,128]{2,1,0:T(8,128)S(1)}, u32[]{:S(2)}, u32[]{:S(2)}) collective-permute-start(f32[2,128,128]{2,1,0:T(8,128)S(1)} %multiply_add_fusion.10), channel_id=1, source_target_pairs={{0,32},{32,64},{64,96},{96,128},{128,160},{160,192},{192,224},{224... | collective-permute-start | bytes 393224 | tf_op jit(solution)/shard_map/while/body/eval_jaxpr/ppermute | solution.py:13
  109.8 5.6 %collective-permute-start = (f32[2,128,128]{2,1,0:T(8,128)S(1)}, f32[2,128,128]{2,1,0:T(8,128)S(1)}, u32[]{:S(2)}, u32[]{:S(2)}) collective-permute-start(f32[2,128,128]{2,1,0:T(8,128)S(1)} %multiply_add_fusion.10), channel_id=1, source_target_pairs={{0,32},{32,64},{64,96},{96,128},{128,160},{160,192},{192,224},{224... | collective-permute-start | bytes 393224 | tf_op jit(solution)/shard_map/while/body/eval_jaxpr/ppermute | solution.py:13
  139.9 62.7 %psum.21 = f32[1024]{0:T(1024)S(1)} all-reduce(f32[1024]{0:T(1024)S(1)} %bitcast.231), channel_id=1, replica_groups=mesh['seq'=16,'head'=32] {'head'}, use_global_device_ids=true, to_apply=%region_6.7 | all-reduce | flops 1024 | bytes 8192 | tf_op jit(solution)/shard_map/psum | solution.py:92
  204.7 32.4 %psum.23 = f32[256]{0:T(256)} all-reduce(f32[256]{0:T(256)S(1)} %get-tuple-element.107), channel_id=1, replica_groups=mesh['seq'=16,'head'=32] {'seq'}, use_global_device_ids=true, to_apply=%region_12.13 | all-reduce | flops 256 | bytes 2048 | tf_op jit(solution)/shard_map/psum | solution.py:133
  237.2 62.7 %psum.22 = f32[1024]{0:T(1024)S(1)} all-reduce(f32[1024]{0:T(1024)S(1)} %get-tuple-element.108), channel_id=1, replica_groups=mesh['seq'=16,'head'=32] {'head'}, use_global_device_ids=true, to_apply=%region_8.9 | all-reduce | flops 1024 | bytes 8192 | tf_op jit(solution)/shard_map/psum | solution.py:95
  303.1 6.1 %convolution_bitcast_fusion.4 = f32[4,256,2,128]{3,1,0,2:T(8,128)} fusion(f32[2,4,256,256]{3,2,1,0:T(8,128)} %copy-done, f32[4,256,2,128]{3,2,1,0:T(2,128)S(1)} %reshape.129), kind=kOutput, calls=%fused_computation.11 | convolution fusion | flops 805306368 | bytes 4194304 | tf_op jit(solution)/shard_map/hnij,hnid->hnjd/dot_general | solution.py:108
  310.5 147.5 %while.25 = (s32[]{:T(128)}, f32[2,128,128]{2,1,0:T(8,128)S(1)}, f32[2,1,1]{0,2,1:T(1,128)}, f32[2,128,128]{2,1,0:T(8,128)S(1)}, s32[]{:T(128)}) while((s32[]{:T(128)}, f32[2,128,128]{2,1,0:T(8,128)S(1)}, f32[2,1,1]{0,2,1:T(1,128)}, f32[2,128,128]{2,1,0:T(8,128)S(1)}, s32[]{:T(128)}) %tuple.69), condition=%wide.region_10.11_spmd, body=%wide.region_9.10_spmd.sunk | while | flops 65538 | bytes 917613 | solution.py:41
  314.1 6.6 %collective-permute-done.1 = f32[2,128,128]{2,1,0:T(8,128)S(1)} collective-permute-done((f32[2,128,128]{2,1,0:T(8,128)}, f32[2,128,128]{2,1,0:T(8,128)S(1)}, u32[]{:S(2)}, u32[]{:S(2)}) %collective-permute-start.1) | collective-permute-done | bytes 131104 | tf_op jit(solution)/shard_map/while/body/eval_jaxpr/ppermute | solution.py:13
  324.0 6.4 %collective-permute-done.1 = f32[2,128,128]{2,1,0:T(8,128)S(1)} collective-permute-done((f32[2,128,128]{2,1,0:T(8,128)}, f32[2,128,128]{2,1,0:T(8,128)S(1)}, u32[]{:S(2)}, u32[]{:S(2)}) %collective-permute-start.1) | collective-permute-done | bytes 131104 | tf_op jit(solution)/shard_map/while/body/eval_jaxpr/ppermute | solution.py:13
  333.7 6.4 %collective-permute-done.1 = f32[2,128,128]{2,1,0:T(8,128)S(1)} collective-permute-done((f32[2,128,128]{2,1,0:T(8,128)}, f32[2,128,128]{2,1,0:T(8,128)S(1)}, u32[]{:S(2)}, u32[]{:S(2)}) %collective-permute-start.1) | collective-permute-done | bytes 131104 | tf_op jit(solution)/shard_map/while/body/eval_jaxpr/ppermute | solution.py:13
  343.4 6.4 %collective-permute-done.1 = f32[2,128,128]{2,1,0:T(8,128)S(1)} collective-permute-done((f32[2,128,128]{2,1,0:T(8,128)}, f32[2,128,128]{2,1,0:T(8,128)S(1)}, u32[]{:S(2)}, u32[]{:S(2)}) %collective-permute-start.1) | collective-permute-done | bytes 131104 | tf_op jit(solution)/shard_map/while/body/eval_jaxpr/ppermute | solution.py:13
  353.1 6.4 %collective-permute-done.1 = f32[2,128,128]{2,1,0:T(8,128)S(1)} collective-permute-done((f32[2,128,128]{2,1,0:T(8,128)}, f32[2,128,128]{2,1,0:T(8,128)S(1)}, u32[]{:S(2)}, u32[]{:S(2)}) %collective-permute-start.1) | collective-permute-done | bytes 131104 | tf_op jit(solution)/shard_map/while/body/eval_jaxpr/ppermute | solution.py:13
  362.8 6.4 %collective-permute-done.1 = f32[2,128,128]{2,1,0:T(8,128)S(1)} collective-permute-done((f32[2,128,128]{2,1,0:T(8,128)}, f32[2,128,128]{2,1,0:T(8,128)S(1)}, u32[]{:S(2)}, u32[]{:S(2)}) %collective-permute-start.1) | collective-permute-done | bytes 131104 | tf_op jit(solution)/shard_map/while/body/eval_jaxpr/ppermute | solution.py:13
  372.4 6.9 %collective-permute-done.1 = f32[2,128,128]{2,1,0:T(8,128)S(1)} collective-permute-done((f32[2,128,128]{2,1,0:T(8,128)}, f32[2,128,128]{2,1,0:T(8,128)S(1)}, u32[]{:S(2)}, u32[]{:S(2)}) %collective-permute-start.1) | collective-permute-done | bytes 131104 | tf_op jit(solution)/shard_map/while/body/eval_jaxpr/ppermute | solution.py:13
  382.7 7.4 %collective-permute-done.1 = f32[2,128,128]{2,1,0:T(8,128)S(1)} collective-permute-done((f32[2,128,128]{2,1,0:T(8,128)}, f32[2,128,128]{2,1,0:T(8,128)S(1)}, u32[]{:S(2)}, u32[]{:S(2)}) %collective-permute-start.1) | collective-permute-done | bytes 131104 | tf_op jit(solution)/shard_map/while/body/eval_jaxpr/ppermute | solution.py:13
  393.4 6.6 %collective-permute-done.1 = f32[2,128,128]{2,1,0:T(8,128)S(1)} collective-permute-done((f32[2,128,128]{2,1,0:T(8,128)}, f32[2,128,128]{2,1,0:T(8,128)S(1)}, u32[]{:S(2)}, u32[]{:S(2)}) %collective-permute-start.1) | collective-permute-done | bytes 131104 | tf_op jit(solution)/shard_map/while/body/eval_jaxpr/ppermute | solution.py:13
  403.3 6.4 %collective-permute-done.1 = f32[2,128,128]{2,1,0:T(8,128)S(1)} collective-permute-done((f32[2,128,128]{2,1,0:T(8,128)}, f32[2,128,128]{2,1,0:T(8,128)S(1)}, u32[]{:S(2)}, u32[]{:S(2)}) %collective-permute-start.1) | collective-permute-done | bytes 131104 | tf_op jit(solution)/shard_map/while/body/eval_jaxpr/ppermute | solution.py:13
  413.0 6.4 %collective-permute-done.1 = f32[2,128,128]{2,1,0:T(8,128)S(1)} collective-permute-done((f32[2,128,128]{2,1,0:T(8,128)}, f32[2,128,128]{2,1,0:T(8,128)S(1)}, u32[]{:S(2)}, u32[]{:S(2)}) %collective-permute-start.1) | collective-permute-done | bytes 131104 | tf_op jit(solution)/shard_map/while/body/eval_jaxpr/ppermute | solution.py:13
  422.7 6.4 %collective-permute-done.1 = f32[2,128,128]{2,1,0:T(8,128)S(1)} collective-permute-done((f32[2,128,128]{2,1,0:T(8,128)}, f32[2,128,128]{2,1,0:T(8,128)S(1)}, u32[]{:S(2)}, u32[]{:S(2)}) %collective-permute-start.1) | collective-permute-done | bytes 131104 | tf_op jit(solution)/shard_map/while/body/eval_jaxpr/ppermute | solution.py:13
  432.4 6.4 %collective-permute-done.1 = f32[2,128,128]{2,1,0:T(8,128)S(1)} collective-permute-done((f32[2,128,128]{2,1,0:T(8,128)}, f32[2,128,128]{2,1,0:T(8,128)S(1)}, u32[]{:S(2)}, u32[]{:S(2)}) %collective-permute-start.1) | collective-permute-done | bytes 131104 | tf_op jit(solution)/shard_map/while/body/eval_jaxpr/ppermute | solution.py:13
  442.1 6.4 %collective-permute-done.1 = f32[2,128,128]{2,1,0:T(8,128)S(1)} collective-permute-done((f32[2,128,128]{2,1,0:T(8,128)}, f32[2,128,128]{2,1,0:T(8,128)S(1)}, u32[]{:S(2)}, u32[]{:S(2)}) %collective-permute-start.1) | collective-permute-done | bytes 131104 | tf_op jit(solution)/shard_map/while/body/eval_jaxpr/ppermute | solution.py:13
  451.7 6.4 %collective-permute-done.1 = f32[2,128,128]{2,1,0:T(8,128)S(1)} collective-permute-done((f32[2,128,128]{2,1,0:T(8,128)}, f32[2,128,128]{2,1,0:T(8,128)S(1)}, u32[]{:S(2)}, u32[]{:S(2)}) %collective-permute-start.1) | collective-permute-done | bytes 131104 | tf_op jit(solution)/shard_map/while/body/eval_jaxpr/ppermute | solution.py:13
  (170 shorter events, 191.6 us)
Async XLA Ops:
  17.8 8.1 %collective-permute-start = (f32[2,128,128]{2,1,0:T(8,128)S(1)}, f32[2,128,128]{2,1,0:T(8,128)S(1)}, u32[]{:S(2)}, u32[]{:S(2)}) collective-permute-start(f32[2,128,128]{2,1,0:T(8,128)S(1)} %multiply_add_fusion.10), channel_id=1, source_target_pairs={{0,32},{32,64},{64,96},{96,128},{128,160},{160,192},{192,224},{224... | collective-permute-start | bytes 393224 | tf_op jit(solution)/shard_map/while/body/eval_jaxpr/ppermute | solution.py:13
  42.3 8.1 %collective-permute-start = (f32[2,128,128]{2,1,0:T(8,128)S(1)}, f32[2,128,128]{2,1,0:T(8,128)S(1)}, u32[]{:S(2)}, u32[]{:S(2)}) collective-permute-start(f32[2,128,128]{2,1,0:T(8,128)S(1)} %multiply_add_fusion.10), channel_id=1, source_target_pairs={{0,32},{32,64},{64,96},{96,128},{128,160},{160,192},{192,224},{224... | collective-permute-start | bytes 393224 | tf_op jit(solution)/shard_map/while/body/eval_jaxpr/ppermute | solution.py:13
  50.5 9.0 %collective-permute-start = (f32[2,128,128]{2,1,0:T(8,128)S(1)}, f32[2,128,128]{2,1,0:T(8,128)S(1)}, u32[]{:S(2)}, u32[]{:S(2)}) collective-permute-start(f32[2,128,128]{2,1,0:T(8,128)S(1)} %multiply_add_fusion.10), channel_id=1, source_target_pairs={{0,32},{32,64},{64,96},{96,128},{128,160},{160,192},{192,224},{224... | collective-permute-start | bytes 393224 | tf_op jit(solution)/shard_map/while/body/eval_jaxpr/ppermute | solution.py:13
  59.6 8.7 %collective-permute-start = (f32[2,128,128]{2,1,0:T(8,128)S(1)}, f32[2,128,128]{2,1,0:T(8,128)S(1)}, u32[]{:S(2)}, u32[]{:S(2)}) collective-permute-start(f32[2,128,128]{2,1,0:T(8,128)S(1)} %multiply_add_fusion.10), channel_id=1, source_target_pairs={{0,32},{32,64},{64,96},{96,128},{128,160},{160,192},{192,224},{224... | collective-permute-start | bytes 393224 | tf_op jit(solution)/shard_map/while/body/eval_jaxpr/ppermute | solution.py:13
  68.4 8.1 %collective-permute-start = (f32[2,128,128]{2,1,0:T(8,128)S(1)}, f32[2,128,128]{2,1,0:T(8,128)S(1)}, u32[]{:S(2)}, u32[]{:S(2)}) collective-permute-start(f32[2,128,128]{2,1,0:T(8,128)S(1)} %multiply_add_fusion.10), channel_id=1, source_target_pairs={{0,32},{32,64},{64,96},{96,128},{128,160},{160,192},{192,224},{224... | collective-permute-start | bytes 393224 | tf_op jit(solution)/shard_map/while/body/eval_jaxpr/ppermute | solution.py:13
  92.9 8.1 %collective-permute-start = (f32[2,128,128]{2,1,0:T(8,128)S(1)}, f32[2,128,128]{2,1,0:T(8,128)S(1)}, u32[]{:S(2)}, u32[]{:S(2)}) collective-permute-start(f32[2,128,128]{2,1,0:T(8,128)S(1)} %multiply_add_fusion.10), channel_id=1, source_target_pairs={{0,32},{32,64},{64,96},{96,128},{128,160},{160,192},{192,224},{224... | collective-permute-start | bytes 393224 | tf_op jit(solution)/shard_map/while/body/eval_jaxpr/ppermute | solution.py:13
  101.1 8.6 %collective-permute-start = (f32[2,128,128]{2,1,0:T(8,128)S(1)}, f32[2,128,128]{2,1,0:T(8,128)S(1)}, u32[]{:S(2)}, u32[]{:S(2)}) collective-permute-start(f32[2,128,128]{2,1,0:T(8,128)S(1)} %multiply_add_fusion.10), channel_id=1, source_target_pairs={{0,32},{32,64},{64,96},{96,128},{128,160},{160,192},{192,224},{224... | collective-permute-start | bytes 393224 | tf_op jit(solution)/shard_map/while/body/eval_jaxpr/ppermute | solution.py:13
  109.8 9.2 %collective-permute-start = (f32[2,128,128]{2,1,0:T(8,128)S(1)}, f32[2,128,128]{2,1,0:T(8,128)S(1)}, u32[]{:S(2)}, u32[]{:S(2)}) collective-permute-start(f32[2,128,128]{2,1,0:T(8,128)S(1)} %multiply_add_fusion.10), channel_id=1, source_target_pairs={{0,32},{32,64},{64,96},{96,128},{128,160},{160,192},{192,224},{224... | collective-permute-start | bytes 393224 | tf_op jit(solution)/shard_map/while/body/eval_jaxpr/ppermute | solution.py:13
  119.0 8.1 %collective-permute-start = (f32[2,128,128]{2,1,0:T(8,128)S(1)}, f32[2,128,128]{2,1,0:T(8,128)S(1)}, u32[]{:S(2)}, u32[]{:S(2)}) collective-permute-start(f32[2,128,128]{2,1,0:T(8,128)S(1)} %multiply_add_fusion.10), channel_id=1, source_target_pairs={{0,32},{32,64},{64,96},{96,128},{128,160},{160,192},{192,224},{224... | collective-permute-start | bytes 393224 | tf_op jit(solution)/shard_map/while/body/eval_jaxpr/ppermute | solution.py:13
  312.1 8.6 %collective-permute-start.1 = (f32[2,128,128]{2,1,0:T(8,128)}, f32[2,128,128]{2,1,0:T(8,128)S(1)}, u32[]{:S(2)}, u32[]{:S(2)}) collective-permute-start(f32[2,128,128]{2,1,0:T(8,128)} %multiply_add_fusion.11), channel_id=1, source_target_pairs={{32,0},{64,32},{96,64},{128,96},{160,128},{192,160},{224,192},{256... | collective-permute-start | bytes 393224 | tf_op jit(solution)/shard_map/while/body/eval_jaxpr/ppermute | solution.py:13
  322.1 8.3 %collective-permute-start.1 = (f32[2,128,128]{2,1,0:T(8,128)}, f32[2,128,128]{2,1,0:T(8,128)S(1)}, u32[]{:S(2)}, u32[]{:S(2)}) collective-permute-start(f32[2,128,128]{2,1,0:T(8,128)} %multiply_add_fusion.11), channel_id=1, source_target_pairs={{32,0},{64,32},{96,64},{128,96},{160,128},{192,160},{224,192},{256... | collective-permute-start | bytes 393224 | tf_op jit(solution)/shard_map/while/body/eval_jaxpr/ppermute | solution.py:13
  331.8 8.3 %collective-permute-start.1 = (f32[2,128,128]{2,1,0:T(8,128)}, f32[2,128,128]{2,1,0:T(8,128)S(1)}, u32[]{:S(2)}, u32[]{:S(2)}) collective-permute-start(f32[2,128,128]{2,1,0:T(8,128)} %multiply_add_fusion.11), channel_id=1, source_target_pairs={{32,0},{64,32},{96,64},{128,96},{160,128},{192,160},{224,192},{256... | collective-permute-start | bytes 393224 | tf_op jit(solution)/shard_map/while/body/eval_jaxpr/ppermute | solution.py:13
  341.5 8.3 %collective-permute-start.1 = (f32[2,128,128]{2,1,0:T(8,128)}, f32[2,128,128]{2,1,0:T(8,128)S(1)}, u32[]{:S(2)}, u32[]{:S(2)}) collective-permute-start(f32[2,128,128]{2,1,0:T(8,128)} %multiply_add_fusion.11), channel_id=1, source_target_pairs={{32,0},{64,32},{96,64},{128,96},{160,128},{192,160},{224,192},{256... | collective-permute-start | bytes 393224 | tf_op jit(solution)/shard_map/while/body/eval_jaxpr/ppermute | solution.py:13
  351.2 8.3 %collective-permute-start.1 = (f32[2,128,128]{2,1,0:T(8,128)}, f32[2,128,128]{2,1,0:T(8,128)S(1)}, u32[]{:S(2)}, u32[]{:S(2)}) collective-permute-start(f32[2,128,128]{2,1,0:T(8,128)} %multiply_add_fusion.11), channel_id=1, source_target_pairs={{32,0},{64,32},{96,64},{128,96},{160,128},{192,160},{224,192},{256... | collective-permute-start | bytes 393224 | tf_op jit(solution)/shard_map/while/body/eval_jaxpr/ppermute | solution.py:13
  360.8 8.3 %collective-permute-start.1 = (f32[2,128,128]{2,1,0:T(8,128)}, f32[2,128,128]{2,1,0:T(8,128)S(1)}, u32[]{:S(2)}, u32[]{:S(2)}) collective-permute-start(f32[2,128,128]{2,1,0:T(8,128)} %multiply_add_fusion.11), channel_id=1, source_target_pairs={{32,0},{64,32},{96,64},{128,96},{160,128},{192,160},{224,192},{256... | collective-permute-start | bytes 393224 | tf_op jit(solution)/shard_map/while/body/eval_jaxpr/ppermute | solution.py:13
  370.5 8.9 %collective-permute-start.1 = (f32[2,128,128]{2,1,0:T(8,128)}, f32[2,128,128]{2,1,0:T(8,128)S(1)}, u32[]{:S(2)}, u32[]{:S(2)}) collective-permute-start(f32[2,128,128]{2,1,0:T(8,128)} %multiply_add_fusion.11), channel_id=1, source_target_pairs={{32,0},{64,32},{96,64},{128,96},{160,128},{192,160},{224,192},{256... | collective-permute-start | bytes 393224 | tf_op jit(solution)/shard_map/while/body/eval_jaxpr/ppermute | solution.py:13
  380.8 9.3 %collective-permute-start.1 = (f32[2,128,128]{2,1,0:T(8,128)}, f32[2,128,128]{2,1,0:T(8,128)S(1)}, u32[]{:S(2)}, u32[]{:S(2)}) collective-permute-start(f32[2,128,128]{2,1,0:T(8,128)} %multiply_add_fusion.11), channel_id=1, source_target_pairs={{32,0},{64,32},{96,64},{128,96},{160,128},{192,160},{224,192},{256... | collective-permute-start | bytes 393224 | tf_op jit(solution)/shard_map/while/body/eval_jaxpr/ppermute | solution.py:13
  391.5 8.5 %collective-permute-start.1 = (f32[2,128,128]{2,1,0:T(8,128)}, f32[2,128,128]{2,1,0:T(8,128)S(1)}, u32[]{:S(2)}, u32[]{:S(2)}) collective-permute-start(f32[2,128,128]{2,1,0:T(8,128)} %multiply_add_fusion.11), channel_id=1, source_target_pairs={{32,0},{64,32},{96,64},{128,96},{160,128},{192,160},{224,192},{256... | collective-permute-start | bytes 393224 | tf_op jit(solution)/shard_map/while/body/eval_jaxpr/ppermute | solution.py:13
  401.4 8.3 %collective-permute-start.1 = (f32[2,128,128]{2,1,0:T(8,128)}, f32[2,128,128]{2,1,0:T(8,128)S(1)}, u32[]{:S(2)}, u32[]{:S(2)}) collective-permute-start(f32[2,128,128]{2,1,0:T(8,128)} %multiply_add_fusion.11), channel_id=1, source_target_pairs={{32,0},{64,32},{96,64},{128,96},{160,128},{192,160},{224,192},{256... | collective-permute-start | bytes 393224 | tf_op jit(solution)/shard_map/while/body/eval_jaxpr/ppermute | solution.py:13
  411.1 8.3 %collective-permute-start.1 = (f32[2,128,128]{2,1,0:T(8,128)}, f32[2,128,128]{2,1,0:T(8,128)S(1)}, u32[]{:S(2)}, u32[]{:S(2)}) collective-permute-start(f32[2,128,128]{2,1,0:T(8,128)} %multiply_add_fusion.11), channel_id=1, source_target_pairs={{32,0},{64,32},{96,64},{128,96},{160,128},{192,160},{224,192},{256... | collective-permute-start | bytes 393224 | tf_op jit(solution)/shard_map/while/body/eval_jaxpr/ppermute | solution.py:13
  420.8 8.3 %collective-permute-start.1 = (f32[2,128,128]{2,1,0:T(8,128)}, f32[2,128,128]{2,1,0:T(8,128)S(1)}, u32[]{:S(2)}, u32[]{:S(2)}) collective-permute-start(f32[2,128,128]{2,1,0:T(8,128)} %multiply_add_fusion.11), channel_id=1, source_target_pairs={{32,0},{64,32},{96,64},{128,96},{160,128},{192,160},{224,192},{256... | collective-permute-start | bytes 393224 | tf_op jit(solution)/shard_map/while/body/eval_jaxpr/ppermute | solution.py:13
  430.5 8.3 %collective-permute-start.1 = (f32[2,128,128]{2,1,0:T(8,128)}, f32[2,128,128]{2,1,0:T(8,128)S(1)}, u32[]{:S(2)}, u32[]{:S(2)}) collective-permute-start(f32[2,128,128]{2,1,0:T(8,128)} %multiply_add_fusion.11), channel_id=1, source_target_pairs={{32,0},{64,32},{96,64},{128,96},{160,128},{192,160},{224,192},{256... | collective-permute-start | bytes 393224 | tf_op jit(solution)/shard_map/while/body/eval_jaxpr/ppermute | solution.py:13
  440.1 8.3 %collective-permute-start.1 = (f32[2,128,128]{2,1,0:T(8,128)}, f32[2,128,128]{2,1,0:T(8,128)S(1)}, u32[]{:S(2)}, u32[]{:S(2)}) collective-permute-start(f32[2,128,128]{2,1,0:T(8,128)} %multiply_add_fusion.11), channel_id=1, source_target_pairs={{32,0},{64,32},{96,64},{128,96},{160,128},{192,160},{224,192},{256... | collective-permute-start | bytes 393224 | tf_op jit(solution)/shard_map/while/body/eval_jaxpr/ppermute | solution.py:13
  449.8 8.3 %collective-permute-start.1 = (f32[2,128,128]{2,1,0:T(8,128)}, f32[2,128,128]{2,1,0:T(8,128)S(1)}, u32[]{:S(2)}, u32[]{:S(2)}) collective-permute-start(f32[2,128,128]{2,1,0:T(8,128)} %multiply_add_fusion.11), channel_id=1, source_target_pairs={{32,0},{64,32},{96,64},{128,96},{160,128},{192,160},{224,192},{256... | collective-permute-start | bytes 393224 | tf_op jit(solution)/shard_map/while/body/eval_jaxpr/ppermute | solution.py:13
  (30 other events, 869.6 us)
where the time goes:
time: 473 us; the launch traced here: 471 us
  blocking collectives  158 us (33%)
  waiting for transfers between devices  138 us (29%)
  starting transfers between devices  112 us (24%)
  other arithmetic  29.4 us (6%)
  matrix products  20.7 us (4%)
  local copies, waits for them, and re-layouts  11.8 us (2%)
    ppermute x30, waiting for transfers between devices, passed_along(): lax.ppermute(value, axis, [(source, source + steps) for source in range(i...  138 us
    ppermute x30, starting transfers between devices, passed_along(): lax.ppermute(value, axis, [(source, source + steps) for source in range(i...  112 us
    psum x1, blocking collectives, local(): squares = lax.psum(jnp.sum(flattened * flattened, axis=1), 'head')  62.7 us
    psum x1, blocking collectives, local(): projected = lax.psum(jnp.sum(normed_grad * normed, axis=1), 'head')  62.7 us
    psum x1, blocking collectives, local(): gain_grad = lax.psum(gain_part, 'seq')  32.4 us
    add x15, other arithmetic, relay_step(): outgoing = jnp.exp(device_decay)[:, None, None] * suffix + device_back  21.1 us
  transfers between devices with their start and end apart: 30, of which 30 were waited for; matrix products, arithmetic and copies ran while one was open for 0% of the time, Pallas kernels for 0%

commit v1 on v0

--- a/solution.py
+++ b/solution.py
@@ -92,7 +92,7 @@
     squares = lax.psum(jnp.sum(flattened * flattened, axis=1), "head")
     inverse = 1.0 / jnp.sqrt(squares / total_channels + epsilon)
     normed = flattened * inverse[:, None]
-    projected = lax.psum(jnp.sum(normed_grad * normed, axis=1), "head")
+    projected = jnp.sum(lax.all_gather(jnp.sum(normed_grad * normed, axis=1), "head"), axis=0)
     output = (normed * gain).astype(jnp.bfloat16)
     gain_part = jnp.sum(grad_wide * normed, axis=0)
     flat_grad = (normed_grad - normed * (projected / total_channels)[:, None]) * inverse[:, None]

time: 473 us -> 434 us (0.918)
  the two profiles are of different devices: /device:TPU:96 before, /device:TPU:98 now
where the time goes in v1:
time: 434 us; the launch traced here: 433 us
  waiting for transfers between devices  139 us (32%)
  blocking collectives  117 us (27%)
  starting transfers between devices  112 us (26%)
  other arithmetic  30.2 us (7%)
  matrix products  20.7 us (5%)
  local copies, waits for them, and re-layouts  11.9 us (3%)
    ppermute x30, waiting for transfers between devices, passed_along(): lax.ppermute(value, axis, [(source, source + steps) for source in range(i...  139 us
    ppermute x30, starting transfers between devices, passed_along(): lax.ppermute(value, axis, [(source, source + steps) for source in range(i...  112 us
    psum x1, blocking collectives, local(): squares = lax.psum(jnp.sum(flattened * flattened, axis=1), 'head')  53 us
    psum x1, blocking collectives, local(): gain_grad = lax.psum(gain_part, 'seq')  32.4 us
    all_gather x1, blocking collectives, local(): lax.all_gather(jnp.sum(normed_grad * normed, axis=1), 'head')  32 us
    add x15, other arithmetic, relay_step(): outgoing = jnp.exp(device_decay)[:, None, None] * suffix + device_back  21.2 us
  transfers between devices with their start and end apart: 30, of which 30 were waited for; matrix products, arithmetic and copies ran while one was open for 0% of the time, Pallas kernels for 0%

profile of v1, /device:TPU:98, one launch (start us, length us, event | category | flops | bytes accessed | tf_op | source)
XLA Modules:
  0.0 432.5 jit_solution(11748013301325978053)
XLA Ops:
  9.9 125.4 %while.24 = (s32[]{:T(128)}, f32[2,128,128]{2,1,0:T(8,128)S(1)}, f32[2,1,1]{0,2,1:T(1,128)S(1)}, f32[2,128,128]{2,1,0:T(8,128)S(1)}, s32[]{:T(128)}) while((s32[]{:T(128)}, f32[2,128,128]{2,1,0:T(8,128)S(1)}, f32[2,1,1]{0,2,1:T(1,128)S(1)}, f32[2,128,128]{2,1,0:T(8,128)S(1)}, s32[]{:T(128)}) %tuple.63), condition=%wide.region_4.5_spmd, body=%wide.region_3.4_spmd.sunk | while | flops 65538 | bytes 917613 | solution.py:32
  59.6 5.6 %collective-permute-start = (f32[2,128,128]{2,1,0:T(8,128)S(1)}, f32[2,128,128]{2,1,0:T(8,128)S(1)}, u32[]{:S(2)}, u32[]{:S(2)}) collective-permute-start(f32[2,128,128]{2,1,0:T(8,128)S(1)} %multiply_add_fusion.10), channel_id=1, source_target_pairs={{0,32},{32,64},{64,96},{96,128},{128,160},{160,192},{192,224},{224... | collective-permute-start | bytes 393224 | tf_op jit(solution)/shard_map/while/body/eval_jaxpr/ppermute | solution.py:13
  68.4 5.6 %collective-permute-start = (f32[2,128,128]{2,1,0:T(8,128)S(1)}, f32[2,128,128]{2,1,0:T(8,128)S(1)}, u32[]{:S(2)}, u32[]{:S(2)}) collective-permute-start(f32[2,128,128]{2,1,0:T(8,128)S(1)} %multiply_add_fusion.10), channel_id=1, source_target_pairs={{0,32},{32,64},{64,96},{96,128},{128,160},{160,192},{192,224},{224... | collective-permute-start | bytes 393224 | tf_op jit(solution)/shard_map/while/body/eval_jaxpr/ppermute | solution.py:13
  119.0 5.6 %collective-permute-start = (f32[2,128,128]{2,1,0:T(8,128)S(1)}, f32[2,128,128]{2,1,0:T(8,128)S(1)}, u32[]{:S(2)}, u32[]{:S(2)}) collective-permute-start(f32[2,128,128]{2,1,0:T(8,128)S(1)} %multiply_add_fusion.10), channel_id=1, source_target_pairs={{0,32},{32,64},{64,96},{96,128},{128,160},{160,192},{192,224},{224... | collective-permute-start | bytes 393224 | tf_op jit(solution)/shard_map/while/body/eval_jaxpr/ppermute | solution.py:13
  139.9 53.0 %psum.14 = f32[1024]{0:T(1024)S(1)} all-reduce(f32[1024]{0:T(1024)S(1)} %bitcast.231), channel_id=1, replica_groups=mesh['seq'=16,'head'=32] {'head'}, use_global_device_ids=true, to_apply=%region_6.7 | all-reduce | flops 1024 | bytes 8192 | tf_op jit(solution)/shard_map/psum | solution.py:92
  195.1 32.4 %psum.15 = f32[256]{0:T(256)} all-reduce(f32[256]{0:T(256)S(1)} %get-tuple-element.107), channel_id=1, replica_groups=mesh['seq'=16,'head'=32] {'seq'}, use_global_device_ids=true, to_apply=%region_12.13 | all-reduce | flops 256 | bytes 2048 | tf_op jit(solution)/shard_map/psum | solution.py:133
  227.5 32.0 %all-gather = f32[32768]{0:T(1024)S(1)} all-gather(f32[1024]{0:T(1024)S(1)} %get-tuple-element.108), channel_id=2, replica_groups=mesh['seq'=16,'head'=32] {'head'}, dimensions={0}, use_global_device_ids=true | all-gather | bytes 135168 | tf_op jit(solution)/shard_map/all_gather | solution.py:95
  263.5 6.1 %convolution_bitcast_fusion.4 = f32[4,256,2,128]{3,1,0,2:T(8,128)} fusion(f32[2,4,256,256]{3,2,1,0:T(8,128)} %copy-done, f32[4,256,2,128]{3,2,1,0:T(2,128)S(1)} %reshape.131), kind=kOutput, calls=%fused_computation.11 | convolution fusion | flops 805306368 | bytes 4194304 | tf_op jit(solution)/shard_map/hnij,hnid->hnjd/dot_general | solution.py:108
  271.0 148.2 %while.25 = (s32[]{:T(128)}, f32[2,128,128]{2,1,0:T(8,128)S(1)}, f32[2,1,1]{0,2,1:T(1,128)}, f32[2,128,128]{2,1,0:T(8,128)S(1)}, s32[]{:T(128)}) while((s32[]{:T(128)}, f32[2,128,128]{2,1,0:T(8,128)S(1)}, f32[2,1,1]{0,2,1:T(1,128)}, f32[2,128,128]{2,1,0:T(8,128)S(1)}, s32[]{:T(128)}) %tuple.69), condition=%wide.region_10.11_spmd, body=%wide.region_9.10_spmd.sunk | while | flops 65538 | bytes 917613 | solution.py:41
  274.5 7.1 %collective-permute-done.1 = f32[2,128,128]{2,1,0:T(8,128)S(1)} collective-permute-done((f32[2,128,128]{2,1,0:T(8,128)}, f32[2,128,128]{2,1,0:T(8,128)S(1)}, u32[]{:S(2)}, u32[]{:S(2)}) %collective-permute-start.1) | collective-permute-done | bytes 131104 | tf_op jit(solution)/shard_map/while/body/eval_jaxpr/ppermute | solution.py:13
  285.0 6.4 %collective-permute-done.1 = f32[2,128,128]{2,1,0:T(8,128)S(1)} collective-permute-done((f32[2,128,128]{2,1,0:T(8,128)}, f32[2,128,128]{2,1,0:T(8,128)S(1)}, u32[]{:S(2)}, u32[]{:S(2)}) %collective-permute-start.1) | collective-permute-done | bytes 131104 | tf_op jit(solution)/shard_map/while/body/eval_jaxpr/ppermute | solution.py:13
  294.7 6.4 %collective-permute-done.1 = f32[2,128,128]{2,1,0:T(8,128)S(1)} collective-permute-done((f32[2,128,128]{2,1,0:T(8,128)}, f32[2,128,128]{2,1,0:T(8,128)S(1)}, u32[]{:S(2)}, u32[]{:S(2)}) %collective-permute-start.1) | collective-permute-done | bytes 131104 | tf_op jit(solution)/shard_map/while/body/eval_jaxpr/ppermute | solution.py:13
  304.4 6.4 %collective-permute-done.1 = f32[2,128,128]{2,1,0:T(8,128)S(1)} collective-permute-done((f32[2,128,128]{2,1,0:T(8,128)}, f32[2,128,128]{2,1,0:T(8,128)S(1)}, u32[]{:S(2)}, u32[]{:S(2)}) %collective-permute-start.1) | collective-permute-done | bytes 131104 | tf_op jit(solution)/shard_map/while/body/eval_jaxpr/ppermute | solution.py:13
  314.1 6.4 %collective-permute-done.1 = f32[2,128,128]{2,1,0:T(8,128)S(1)} collective-permute-done((f32[2,128,128]{2,1,0:T(8,128)}, f32[2,128,128]{2,1,0:T(8,128)S(1)}, u32[]{:S(2)}, u32[]{:S(2)}) %collective-permute-start.1) | collective-permute-done | bytes 131104 | tf_op jit(solution)/shard_map/while/body/eval_jaxpr/ppermute | solution.py:13
  323.8 6.4 %collective-permute-done.1 = f32[2,128,128]{2,1,0:T(8,128)S(1)} collective-permute-done((f32[2,128,128]{2,1,0:T(8,128)}, f32[2,128,128]{2,1,0:T(8,128)S(1)}, u32[]{:S(2)}, u32[]{:S(2)}) %collective-permute-start.1) | collective-permute-done | bytes 131104 | tf_op jit(solution)/shard_map/while/body/eval_jaxpr/ppermute | solution.py:13
  333.4 6.4 %collective-permute-done.1 = f32[2,128,128]{2,1,0:T(8,128)S(1)} collective-permute-done((f32[2,128,128]{2,1,0:T(8,128)}, f32[2,128,128]{2,1,0:T(8,128)S(1)}, u32[]{:S(2)}, u32[]{:S(2)}) %collective-permute-start.1) | collective-permute-done | bytes 131104 | tf_op jit(solution)/shard_map/while/body/eval_jaxpr/ppermute | solution.py:13
  343.2 7.6 %collective-permute-done.1 = f32[2,128,128]{2,1,0:T(8,128)S(1)} collective-permute-done((f32[2,128,128]{2,1,0:T(8,128)}, f32[2,128,128]{2,1,0:T(8,128)S(1)}, u32[]{:S(2)}, u32[]{:S(2)}) %collective-permute-start.1) | collective-permute-done | bytes 131104 | tf_op jit(solution)/shard_map/while/body/eval_jaxpr/ppermute | solution.py:13
  354.2 6.9 %collective-permute-done.1 = f32[2,128,128]{2,1,0:T(8,128)S(1)} collective-permute-done((f32[2,128,128]{2,1,0:T(8,128)}, f32[2,128,128]{2,1,0:T(8,128)S(1)}, u32[]{:S(2)}, u32[]{:S(2)}) %collective-permute-start.1) | collective-permute-done | bytes 131104 | tf_op jit(solution)/shard_map/while/body/eval_jaxpr/ppermute | solution.py:13
  364.4 6.4 %collective-permute-done.1 = f32[2,128,128]{2,1,0:T(8,128)S(1)} collective-permute-done((f32[2,128,128]{2,1,0:T(8,128)}, f32[2,128,128]{2,1,0:T(8,128)S(1)}, u32[]{:S(2)}, u32[]{:S(2)}) %collective-permute-start.1) | collective-permute-done | bytes 131104 | tf_op jit(solution)/shard_map/while/body/eval_jaxpr/ppermute | solution.py:13
  374.1 6.4 %collective-permute-done.1 = f32[2,128,128]{2,1,0:T(8,128)S(1)} collective-permute-done((f32[2,128,128]{2,1,0:T(8,128)}, f32[2,128,128]{2,1,0:T(8,128)S(1)}, u32[]{:S(2)}, u32[]{:S(2)}) %collective-permute-start.1) | collective-permute-done | bytes 131104 | tf_op jit(solution)/shard_map/while/body/eval_jaxpr/ppermute | solution.py:13
  383.8 6.4 %collective-permute-done.1 = f32[2,128,128]{2,1,0:T(8,128)S(1)} collective-permute-done((f32[2,128,128]{2,1,0:T(8,128)}, f32[2,128,128]{2,1,0:T(8,128)S(1)}, u32[]{:S(2)}, u32[]{:S(2)}) %collective-permute-start.1) | collective-permute-done | bytes 131104 | tf_op jit(solution)/shard_map/while/body/eval_jaxpr/ppermute | solution.py:13
  393.5 6.4 %collective-permute-done.1 = f32[2,128,128]{2,1,0:T(8,128)S(1)} collective-permute-done((f32[2,128,128]{2,1,0:T(8,128)}, f32[2,128,128]{2,1,0:T(8,128)S(1)}, u32[]{:S(2)}, u32[]{:S(2)}) %collective-permute-start.1) | collective-permute-done | bytes 131104 | tf_op jit(solution)/shard_map/while/body/eval_jaxpr/ppermute | solution.py:13
  403.1 6.4 %collective-permute-done.1 = f32[2,128,128]{2,1,0:T(8,128)S(1)} collective-permute-done((f32[2,128,128]{2,1,0:T(8,128)}, f32[2,128,128]{2,1,0:T(8,128)S(1)}, u32[]{:S(2)}, u32[]{:S(2)}) %collective-permute-start.1) | collective-permute-done | bytes 131104 | tf_op jit(solution)/shard_map/while/body/eval_jaxpr/ppermute | solution.py:13
  412.8 6.4 %collective-permute-done.1 = f32[2,128,128]{2,1,0:T(8,128)S(1)} collective-permute-done((f32[2,128,128]{2,1,0:T(8,128)}, f32[2,128,128]{2,1,0:T(8,128)S(1)}, u32[]{:S(2)}, u32[]{:S(2)}) %collective-permute-start.1) | collective-permute-done | bytes 131104 | tf_op jit(solution)/shard_map/while/body/eval_jaxpr/ppermute | solution.py:13
  (174 shorter events, 192.5 us)
Async XLA Ops:
  17.8 8.1 %collective-permute-start = (f32[2,128,128]{2,1,0:T(8,128)S(1)}, f32[2,128,128]{2,1,0:T(8,128)S(1)}, u32[]{:S(2)}, u32[]{:S(2)}) collective-permute-start(f32[2,128,128]{2,1,0:T(8,128)S(1)} %multiply_add_fusion.10), channel_id=1, source_target_pairs={{0,32},{32,64},{64,96},{96,128},{128,160},{160,192},{192,224},{224... | collective-permute-start | bytes 393224 | tf_op jit(solution)/shard_map/while/body/eval_jaxpr/ppermute | solution.py:13
  26.0 8.1 %collective-permute-start = (f32[2,128,128]{2,1,0:T(8,128)S(1)}, f32[2,128,128]{2,1,0:T(8,128)S(1)}, u32[]{:S(2)}, u32[]{:S(2)}) collective-permute-start(f32[2,128,128]{2,1,0:T(8,128)S(1)} %multiply_add_fusion.10), channel_id=1, source_target_pairs={{0,32},{32,64},{64,96},{96,128},{128,160},{160,192},{192,224},{224... | collective-permute-start | bytes 393224 | tf_op jit(solution)/shard_map/while/body/eval_jaxpr/ppermute | solution.py:13
  50.5 9.0 %collective-permute-start = (f32[2,128,128]{2,1,0:T(8,128)S(1)}, f32[2,128,128]{2,1,0:T(8,128)S(1)}, u32[]{:S(2)}, u32[]{:S(2)}) collective-permute-start(f32[2,128,128]{2,1,0:T(8,128)S(1)} %multiply_add_fusion.10), channel_id=1, source_target_pairs={{0,32},{32,64},{64,96},{96,128},{128,160},{160,192},{192,224},{224... | collective-permute-start | bytes 393224 | tf_op jit(solution)/shard_map/while/body/eval_jaxpr/ppermute | solution.py:13
  59.6 8.7 %collective-permute-start = (f32[2,128,128]{2,1,0:T(8,128)S(1)}, f32[2,128,128]{2,1,0:T(8,128)S(1)}, u32[]{:S(2)}, u32[]{:S(2)}) collective-permute-start(f32[2,128,128]{2,1,0:T(8,128)S(1)} %multiply_add_fusion.10), channel_id=1, source_target_pairs={{0,32},{32,64},{64,96},{96,128},{128,160},{160,192},{192,224},{224... | collective-permute-start | bytes 393224 | tf_op jit(solution)/shard_map/while/body/eval_jaxpr/ppermute | solution.py:13
  68.4 8.1 %collective-permute-start = (f32[2,128,128]{2,1,0:T(8,128)S(1)}, f32[2,128,128]{2,1,0:T(8,128)S(1)}, u32[]{:S(2)}, u32[]{:S(2)}) collective-permute-start(f32[2,128,128]{2,1,0:T(8,128)S(1)} %multiply_add_fusion.10), channel_id=1, source_target_pairs={{0,32},{32,64},{64,96},{96,128},{128,160},{160,192},{192,224},{224... | collective-permute-start | bytes 393224 | tf_op jit(solution)/shard_map/while/body/eval_jaxpr/ppermute | solution.py:13
  76.6 8.1 %collective-permute-start = (f32[2,128,128]{2,1,0:T(8,128)S(1)}, f32[2,128,128]{2,1,0:T(8,128)S(1)}, u32[]{:S(2)}, u32[]{:S(2)}) collective-permute-start(f32[2,128,128]{2,1,0:T(8,128)S(1)} %multiply_add_fusion.10), channel_id=1, source_target_pairs={{0,32},{32,64},{64,96},{96,128},{128,160},{160,192},{192,224},{224... | collective-permute-start | bytes 393224 | tf_op jit(solution)/shard_map/while/body/eval_jaxpr/ppermute | solution.py:13
  101.1 8.6 %collective-permute-start = (f32[2,128,128]{2,1,0:T(8,128)S(1)}, f32[2,128,128]{2,1,0:T(8,128)S(1)}, u32[]{:S(2)}, u32[]{:S(2)}) collective-permute-start(f32[2,128,128]{2,1,0:T(8,128)S(1)} %multiply_add_fusion.10), channel_id=1, source_target_pairs={{0,32},{32,64},{64,96},{96,128},{128,160},{160,192},{192,224},{224... | collective-permute-start | bytes 393224 | tf_op jit(solution)/shard_map/while/body/eval_jaxpr/ppermute | solution.py:13
  109.8 9.2 %collective-permute-start = (f32[2,128,128]{2,1,0:T(8,128)S(1)}, f32[2,128,128]{2,1,0:T(8,128)S(1)}, u32[]{:S(2)}, u32[]{:S(2)}) collective-permute-start(f32[2,128,128]{2,1,0:T(8,128)S(1)} %multiply_add_fusion.10), channel_id=1, source_target_pairs={{0,32},{32,64},{64,96},{96,128},{128,160},{160,192},{192,224},{224... | collective-permute-start | bytes 393224 | tf_op jit(solution)/shard_map/while/body/eval_jaxpr/ppermute | solution.py:13
  119.0 8.1 %collective-permute-start = (f32[2,128,128]{2,1,0:T(8,128)S(1)}, f32[2,128,128]{2,1,0:T(8,128)S(1)}, u32[]{:S(2)}, u32[]{:S(2)}) collective-permute-start(f32[2,128,128]{2,1,0:T(8,128)S(1)} %multiply_add_fusion.10), channel_id=1, source_target_pairs={{0,32},{32,64},{64,96},{96,128},{128,160},{160,192},{192,224},{224... | collective-permute-start | bytes 393224 | tf_op jit(solution)/shard_map/while/body/eval_jaxpr/ppermute | solution.py:13
  272.6 9.0 %collective-permute-start.1 = (f32[2,128,128]{2,1,0:T(8,128)}, f32[2,128,128]{2,1,0:T(8,128)S(1)}, u32[]{:S(2)}, u32[]{:S(2)}) collective-permute-start(f32[2,128,128]{2,1,0:T(8,128)} %multiply_add_fusion.11), channel_id=1, source_target_pairs={{32,0},{64,32},{96,64},{128,96},{160,128},{192,160},{224,192},{256... | collective-permute-start | bytes 393224 | tf_op jit(solution)/shard_map/while/body/eval_jaxpr/ppermute | solution.py:13
  283.1 8.3 %collective-permute-start.1 = (f32[2,128,128]{2,1,0:T(8,128)}, f32[2,128,128]{2,1,0:T(8,128)S(1)}, u32[]{:S(2)}, u32[]{:S(2)}) collective-permute-start(f32[2,128,128]{2,1,0:T(8,128)} %multiply_add_fusion.11), channel_id=1, source_target_pairs={{32,0},{64,32},{96,64},{128,96},{160,128},{192,160},{224,192},{256... | collective-permute-start | bytes 393224 | tf_op jit(solution)/shard_map/while/body/eval_jaxpr/ppermute | solution.py:13
  292.8 8.3 %collective-permute-start.1 = (f32[2,128,128]{2,1,0:T(8,128)}, f32[2,128,128]{2,1,0:T(8,128)S(1)}, u32[]{:S(2)}, u32[]{:S(2)}) collective-permute-start(f32[2,128,128]{2,1,0:T(8,128)} %multiply_add_fusion.11), channel_id=1, source_target_pairs={{32,0},{64,32},{96,64},{128,96},{160,128},{192,160},{224,192},{256... | collective-permute-start | bytes 393224 | tf_op jit(solution)/shard_map/while/body/eval_jaxpr/ppermute | solution.py:13
  302.5 8.3 %collective-permute-start.1 = (f32[2,128,128]{2,1,0:T(8,128)}, f32[2,128,128]{2,1,0:T(8,128)S(1)}, u32[]{:S(2)}, u32[]{:S(2)}) collective-permute-start(f32[2,128,128]{2,1,0:T(8,128)} %multiply_add_fusion.11), channel_id=1, source_target_pairs={{32,0},{64,32},{96,64},{128,96},{160,128},{192,160},{224,192},{256... | collective-permute-start | bytes 393224 | tf_op jit(solution)/shard_map/while/body/eval_jaxpr/ppermute | solution.py:13
  312.1 8.3 %collective-permute-start.1 = (f32[2,128,128]{2,1,0:T(8,128)}, f32[2,128,128]{2,1,0:T(8,128)S(1)}, u32[]{:S(2)}, u32[]{:S(2)}) collective-permute-start(f32[2,128,128]{2,1,0:T(8,128)} %multiply_add_fusion.11), channel_id=1, source_target_pairs={{32,0},{64,32},{96,64},{128,96},{160,128},{192,160},{224,192},{256... | collective-permute-start | bytes 393224 | tf_op jit(solution)/shard_map/while/body/eval_jaxpr/ppermute | solution.py:13
  321.8 8.3 %collective-permute-start.1 = (f32[2,128,128]{2,1,0:T(8,128)}, f32[2,128,128]{2,1,0:T(8,128)S(1)}, u32[]{:S(2)}, u32[]{:S(2)}) collective-permute-start(f32[2,128,128]{2,1,0:T(8,128)} %multiply_add_fusion.11), channel_id=1, source_target_pairs={{32,0},{64,32},{96,64},{128,96},{160,128},{192,160},{224,192},{256... | collective-permute-start | bytes 393224 | tf_op jit(solution)/shard_map/while/body/eval_jaxpr/ppermute | solution.py:13
  331.5 8.4 %collective-permute-start.1 = (f32[2,128,128]{2,1,0:T(8,128)}, f32[2,128,128]{2,1,0:T(8,128)S(1)}, u32[]{:S(2)}, u32[]{:S(2)}) collective-permute-start(f32[2,128,128]{2,1,0:T(8,128)} %multiply_add_fusion.11), channel_id=1, source_target_pairs={{32,0},{64,32},{96,64},{128,96},{160,128},{192,160},{224,192},{256... | collective-permute-start | bytes 393224 | tf_op jit(solution)/shard_map/while/body/eval_jaxpr/ppermute | solution.py:13
  341.3 9.5 %collective-permute-start.1 = (f32[2,128,128]{2,1,0:T(8,128)}, f32[2,128,128]{2,1,0:T(8,128)S(1)}, u32[]{:S(2)}, u32[]{:S(2)}) collective-permute-start(f32[2,128,128]{2,1,0:T(8,128)} %multiply_add_fusion.11), channel_id=1, source_target_pairs={{32,0},{64,32},{96,64},{128,96},{160,128},{192,160},{224,192},{256... | collective-permute-start | bytes 393224 | tf_op jit(solution)/shard_map/while/body/eval_jaxpr/ppermute | solution.py:13
  352.2 8.8 %collective-permute-start.1 = (f32[2,128,128]{2,1,0:T(8,128)}, f32[2,128,128]{2,1,0:T(8,128)S(1)}, u32[]{:S(2)}, u32[]{:S(2)}) collective-permute-start(f32[2,128,128]{2,1,0:T(8,128)} %multiply_add_fusion.11), channel_id=1, source_target_pairs={{32,0},{64,32},{96,64},{128,96},{160,128},{192,160},{224,192},{256... | collective-permute-start | bytes 393224 | tf_op jit(solution)/shard_map/while/body/eval_jaxpr/ppermute | solution.py:13
  362.5 8.3 %collective-permute-start.1 = (f32[2,128,128]{2,1,0:T(8,128)}, f32[2,128,128]{2,1,0:T(8,128)S(1)}, u32[]{:S(2)}, u32[]{:S(2)}) collective-permute-start(f32[2,128,128]{2,1,0:T(8,128)} %multiply_add_fusion.11), channel_id=1, source_target_pairs={{32,0},{64,32},{96,64},{128,96},{160,128},{192,160},{224,192},{256... | collective-permute-start | bytes 393224 | tf_op jit(solution)/shard_map/while/body/eval_jaxpr/ppermute | solution.py:13
  372.2 8.3 %collective-permute-start.1 = (f32[2,128,128]{2,1,0:T(8,128)}, f32[2,128,128]{2,1,0:T(8,128)S(1)}, u32[]{:S(2)}, u32[]{:S(2)}) collective-permute-start(f32[2,128,128]{2,1,0:T(8,128)} %multiply_add_fusion.11), channel_id=1, source_target_pairs={{32,0},{64,32},{96,64},{128,96},{160,128},{192,160},{224,192},{256... | collective-permute-start | bytes 393224 | tf_op jit(solution)/shard_map/while/body/eval_jaxpr/ppermute | solution.py:13
  381.8 8.3 %collective-permute-start.1 = (f32[2,128,128]{2,1,0:T(8,128)}, f32[2,128,128]{2,1,0:T(8,128)S(1)}, u32[]{:S(2)}, u32[]{:S(2)}) collective-permute-start(f32[2,128,128]{2,1,0:T(8,128)} %multiply_add_fusion.11), channel_id=1, source_target_pairs={{32,0},{64,32},{96,64},{128,96},{160,128},{192,160},{224,192},{256... | collective-permute-start | bytes 393224 | tf_op jit(solution)/shard_map/while/body/eval_jaxpr/ppermute | solution.py:13
  391.5 8.3 %collective-permute-start.1 = (f32[2,128,128]{2,1,0:T(8,128)}, f32[2,128,128]{2,1,0:T(8,128)S(1)}, u32[]{:S(2)}, u32[]{:S(2)}) collective-permute-start(f32[2,128,128]{2,1,0:T(8,128)} %multiply_add_fusion.11), channel_id=1, source_target_pairs={{32,0},{64,32},{96,64},{128,96},{160,128},{192,160},{224,192},{256... | collective-permute-start | bytes 393224 | tf_op jit(solution)/shard_map/while/body/eval_jaxpr/ppermute | solution.py:13
  401.2 8.3 %collective-permute-start.1 = (f32[2,128,128]{2,1,0:T(8,128)}, f32[2,128,128]{2,1,0:T(8,128)S(1)}, u32[]{:S(2)}, u32[]{:S(2)}) collective-permute-start(f32[2,128,128]{2,1,0:T(8,128)} %multiply_add_fusion.11), channel_id=1, source_target_pairs={{32,0},{64,32},{96,64},{128,96},{160,128},{192,160},{224,192},{256... | collective-permute-start | bytes 393224 | tf_op jit(solution)/shard_map/while/body/eval_jaxpr/ppermute | solution.py:13
  410.9 8.3 %collective-permute-start.1 = (f32[2,128,128]{2,1,0:T(8,128)}, f32[2,128,128]{2,1,0:T(8,128)S(1)}, u32[]{:S(2)}, u32[]{:S(2)}) collective-permute-start(f32[2,128,128]{2,1,0:T(8,128)} %multiply_add_fusion.11), channel_id=1, source_target_pairs={{32,0},{64,32},{96,64},{128,96},{160,128},{192,160},{224,192},{256... | collective-permute-start | bytes 393224 | tf_op jit(solution)/shard_map/while/body/eval_jaxpr/ppermute | solution.py:13
  (31 other events, 852.4 us)
